TPU v7x, 32 devices: a whole 2x2x4 slice. The times are simulated.
32 devices in a mesh: dp: 4 (over y, core), seq: 8 (over z, x).
Axes of the slice: x: 2, y: 2, z: 4, core: 2. Of those that a mesh axis runs over, the one named last changes fastest.
Arguments:
- query: bfloat16 [8, 2048, 32, 128], P('dp', 'seq'), may hold values from -128 to 128
- keys: bfloat16 [8, 2048, 4, 128], P('dp', 'seq'), may hold values from -4.5 to 4.5
- values: bfloat16 [8, 2048, 4, 128], P('dp', 'seq'), may hold values from -6 to 6
- output: bfloat16 [8, 2048, 32, 128], P('dp', 'seq'), may hold values from -6 to 6
- out_grad: bfloat16 [8, 2048, 32, 128], P('dp', 'seq'), may hold values from -6 to 6
- lengths: int32 [8], P('dp'), may hold values from 341 to 2048, as said below
- margins: float32 [4], P('dp'), may hold values from -3 to 3
Outputs:
- query_grad: bfloat16 [8, 2048, 32, 128], P('dp', 'seq')
- key_grad: bfloat16 [8, 2048, 4, 128], P('dp', 'seq')
- value_grad: bfloat16 [8, 2048, 4, 128], P('dp', 'seq')
Inputs may be any that keep to these rules, and one draw needn't show every extreme that they name: `lengths`: sequence 2p is pair p's chosen response and 2p + 1 its rejected one; some sequence has exactly 2048 tokens.
All inputs are finite; a program needn't handle non-finite values.
Results may differ from a plain program's by a relative error of at most 0.009.
Values may be sent and summed in bfloat16 or wider, within the bound.
A program may use at most 128 MiB of HBM per device.

v0:
```python
import math
import jax
import jax.numpy as jnp
from jax import lax
from jax.sharding import PartitionSpec as P


def sequence_grads(query, scaled, keys, values, delta, length):
    full_len, per_dev, head_dim = query.shape
    slots = keys.shape[1]
    repeat = per_dev // slots
    block = min(512, full_len)
    scale = 1.0 / math.sqrt(head_dim)
    q_four = query.reshape(full_len, slots, repeat, head_dim)
    g_four = scaled.reshape(full_len, slots, repeat, head_dim)
    d_three = delta.reshape(full_len, slots, repeat)

    def make_step(start):
        prefix = start + block

        def one_block(carry):
            query_all, key_acc, value_acc = carry
            q_block = q_four[start:prefix]
            g_block = g_four[start:prefix]
            d_block = jnp.transpose(d_three[start:prefix], (1, 2, 0))[..., None]
            key_pre = keys[:prefix]
            value_pre = values[:prefix]
            scores = (
                jnp.einsum("isrd,jsd->srij", q_block, key_pre, preferred_element_type=jnp.float32)
                * scale
            )
            query_pos = start + jnp.arange(block)
            causal = jnp.arange(prefix)[None, :] <= query_pos[:, None]
            scores = jnp.where(causal, scores, -jnp.inf)
            top = jnp.max(scores, axis=-1, keepdims=True)
            lse = top + jnp.log(jnp.sum(jnp.exp(scores - top), axis=-1, keepdims=True))
            prob = jnp.exp(scores - lse)
            prob_low = prob.astype(jnp.bfloat16)
            value_part = jnp.einsum(
                "srij,isrd->jsd", prob_low, g_block, preferred_element_type=jnp.float32
            )
            dprob = jnp.einsum(
                "isrd,jsd->srij", g_block, value_pre, preferred_element_type=jnp.float32
            )
            dscore = prob * (dprob - d_block)
            dscore_low = dscore.astype(jnp.bfloat16)
            query_part = (
                jnp.einsum(
                    "srij,jsd->isrd", dscore_low, key_pre, preferred_element_type=jnp.float32
                )
                * scale
            )
            query_part = query_part.reshape(block, per_dev, head_dim).astype(jnp.bfloat16)
            query_all = lax.dynamic_update_slice_in_dim(query_all, query_part, start, 0)
            key_part = jnp.einsum(
                "srij,isrd->jsd", dscore_low, q_block, preferred_element_type=jnp.float32
            )
            key_acc = key_acc.at[:prefix].add(key_part)
            value_acc = value_acc.at[:prefix].add(value_part)
            return (query_all, key_acc, value_acc)

        return one_block

    carry = (
        jnp.zeros((full_len, per_dev, head_dim), jnp.bfloat16),
        jnp.zeros((full_len, slots, head_dim), jnp.float32),
        jnp.zeros((full_len, slots, head_dim), jnp.float32),
    )
    for index in range(full_len // block):
        start = index * block
        step_fn = make_step(start)
        carry = step_fn(carry)
    query_all, key_acc, value_acc = carry
    return (query_all, key_acc * scale, value_acc)


def body(query, keys, values, output, out_grad, lengths, margins):
    seq_size = lax.axis_size("seq")
    place = lax.axis_index("seq")
    seqs_dev, toks_dev, heads, head_dim = query.shape
    kv_heads = keys.shape[2]
    per_dev = heads // seq_size
    group = heads // kv_heads
    total = lax.psum(jnp.sum(lengths), "dp")
    mean_len = total.astype(jnp.float32) / (seqs_dev * lax.axis_size("dp"))
    weight = jax.nn.sigmoid(-margins)
    signs = jnp.tile(jnp.array([-1.0, 1.0], jnp.float32), margins.shape[0])
    coef = jnp.repeat(weight, 2) * signs * 4.0 * mean_len / lengths.astype(jnp.float32)
    positions = place * toks_dev + jnp.arange(toks_dev)
    live = (positions[None, :] < lengths[:, None]).astype(jnp.float32)
    factor = coef[:, None] * live
    scaled = (out_grad.astype(jnp.float32) * factor[:, :, None, None]).astype(jnp.bfloat16)
    copies = max(1, group // per_dev)
    key_slots = jnp.repeat(keys, copies, axis=2)
    value_slots = jnp.repeat(values, copies, axis=2)
    q_heads, g_heads, o_heads, k_heads, v_heads = (
        lax.all_to_all(query, "seq", split_axis=2, concat_axis=1, tiled=True),
        lax.all_to_all(scaled, "seq", split_axis=2, concat_axis=1, tiled=True),
        lax.all_to_all(output, "seq", split_axis=2, concat_axis=1, tiled=True),
        lax.all_to_all(key_slots, "seq", split_axis=2, concat_axis=1, tiled=True),
        lax.all_to_all(value_slots, "seq", split_axis=2, concat_axis=1, tiled=True),
    )
    delta = jnp.sum(g_heads.astype(jnp.float32) * o_heads.astype(jnp.float32), axis=3)
    query_heads, key_heads, value_heads = lax.map(
        lambda items: sequence_grads(*items), (q_heads, g_heads, k_heads, v_heads, delta, lengths)
    )
    query_grad = lax.all_to_all(query_heads, "seq", split_axis=1, concat_axis=2, tiled=True)
    key_rows, value_rows = (
        lax.all_to_all(key_heads, "seq", split_axis=1, concat_axis=2, tiled=True),
        lax.all_to_all(value_heads, "seq", split_axis=1, concat_axis=2, tiled=True),
    )
    key_grad = jnp.sum(
        key_rows.reshape(seqs_dev, toks_dev, kv_heads, copies, head_dim), axis=3
    ).astype(jnp.bfloat16)
    value_grad = jnp.sum(
        value_rows.reshape(seqs_dev, toks_dev, kv_heads, copies, head_dim), axis=3
    ).astype(jnp.bfloat16)
    return (query_grad, key_grad, value_grad)


def solution(mesh):
    return jax.shard_map(
        body,
        mesh=mesh,
        in_specs=(
            P("dp", "seq", None, None),
            P("dp", "seq", None, None),
            P("dp", "seq", None, None),
            P("dp", "seq", None, None),
            P("dp", "seq", None, None),
            P("dp"),
            P("dp"),
        ),
        out_specs=(
            P("dp", "seq", None, None),
            P("dp", "seq", None, None),
            P("dp", "seq", None, None),
        ),
        check_vma=False,
    )
```

profile of v0, /device:TPU:0, one launch (start us, length us, event | category | flops | bytes accessed | tf_op | source)
XLA Modules:
  0.0 792.0 jit_solution(2441812579054759764)
XLA Ops:
  3.0 7.3 all-to-all-start
  10.4 25.7 %all-to-all-done = bf16[2,256,8,128]{3,1,0,2:T(8,128)(2,1)S(1)} async-done(((bf16[2,256,8,128]{3,1,0,2:T(8,128)(2,1)}), bf16[2,256,8,128]{3,1,0,2:T(8,128)(2,1)S(1)}, u32[]{:S(2)}, u32[]{:S(2)}) %all-to-all-start) | async-done | bytes 1048608 | tf_op jit(solution)/shard_map/all_to_all | solution.py:100
  37.2 3.6 all-to-all-start.2
  41.5 5.6 psum.7
  48.5 5.9 multiply_convert_fusion
  54.4 12.4 %all-to-all-done.2 = bf16[2,256,8,128]{3,1,0,2:T(8,128)(2,1)S(1)} async-done(((bf16[2,256,8,128]{3,1,0,2:T(8,128)(2,1)}), bf16[2,256,8,128]{3,1,0,2:T(8,128)(2,1)S(1)}, u32[]{:S(2)}, u32[]{:S(2)}) %all-to-all-start.2) | async-done | bytes 1048608 | tf_op jit(solution)/shard_map/all_to_all | solution.py:101
  66.8 4.5 all-to-all-start.3
  71.3 5.8 copy.192
  77.2 86.7 %all-to-all-done.3 = bf16[2,256,32,128]{3,1,0,2:T(8,128)(2,1)} async-done(((bf16[2,256,32,128]{3,1,0,2:T(8,128)(2,1)}), bf16[2,256,32,128]{3,1,0,2:T(8,128)(2,1)}, u32[]{:S(2)}, u32[]{:S(2)}) %all-to-all-start.3) | async-done | bytes 4194336 | tf_op jit(solution)/shard_map/all_to_all | solution.py:98
  163.9 4.6 all-to-all-start.1
  168.5 5.8 copy.198
  174.3 86.7 %all-to-all-done.1 = bf16[2,256,32,128]{3,1,0,2:T(8,128)(2,1)} async-done(((bf16[2,256,32,128]{3,1,0,2:T(8,128)(2,1)}), bf16[2,256,32,128]{3,1,0,2:T(8,128)(2,1)}, u32[]{:S(2)}, u32[]{:S(2)}) %all-to-all-start.1) | async-done | bytes 4194336 | tf_op jit(solution)/shard_map/all_to_all | solution.py:97
  261.0 4.5 all-to-all-start.4
  265.7 2.3 copy.195
  268.0 4.7 copy.197
  272.6 4.6 copy.193
  277.2 80.9 %all-to-all-done.4 = bf16[2,256,32,128]{3,1,0,2:T(8,128)(2,1)} async-done(((bf16[2,256,32,128]{3,1,0,2:T(8,128)(2,1)}), bf16[2,256,32,128]{3,1,0,2:T(8,128)(2,1)}, u32[]{:S(2)}, u32[]{:S(2)}) %all-to-all-start.4) | async-done | bytes 4194336 | tf_op jit(solution)/shard_map/all_to_all | solution.py:99
  358.1 5.7 fusion.155
  363.9 221.8 %while.27 = (s32[]{:T(128)}, bf16[2,2048,4,128]{3,2,0,1:T(4,128)(2,1)}, f32[2,2048,1,128]{3,2,0,1:T(1,128)}, f32[2,2048,1,128]{3,2,0,1:T(1,128)}, bf16[2,2048,1,...) while((s32[]{:T(128)}, ...), condition=%wide.region_12.13_spmd, body=%wide.region_3.12_spmd.sunk | while | flops 13606184960 | bytes 444718720 | solution.py:104
  367.2 2.1 fusion.208
  371.6 2.6 fusion.209
  381.9 4.4 fusion.221
  386.3 3.9 fusion.212
  394.4 2.2 fusion.214
  396.6 2.7 exponential_reduce_fusion.10
  399.4 6.2 fusion.222
  405.6 5.7 fusion.215
  411.3 4.4 fusion.226
  415.7 2.9 fusion.216
  418.6 4.8 fusion.217
  423.4 3.8 exponential_reduce_fusion.11
  429.1 11.9 %fusion.223 = f32[1,2048,1,128]{1,3,2,0:T(8,128)} fusion(f32[2048,1,128]{0,2,1:T(8,128)} %fusion.222, f32[2048,512,4]{1,0,2:T(8,128)} %copy-done, f32[4,512]{1,0:T(4,128)S(1)} %log_add_fusion.11, pred[512,2048]{0,1:T(8,128)(4,1)S(1)} %copy-done.3, bf16[2,2048,4,128]{3,1,2,0:T(8,128)(2,1)} %get-tuple-element.461, s32[]{:T(128)S(6)} %copy.272, ...), kind=kOutput, calls=%fused_computation.58.clone.1 | convolution fusion | flops 1090781184 | bytes 20455432 | tf_op jit(solution)/shard_map/while/body/eval_jaxpr/srij,isrd->jsd/dot_general | solution.py:39
  441.0 9.0 %fusion.218 = bf16[4,512,2048]{1,2,0:T(8,128)(2,1)S(1)} fusion(f32[2048,512,4]{1,0,2:T(8,128)} %copy-done, f32[4,512]{1,0:T(4,128)S(1)} %get-tuple-element.420, f32[4,512]{1,0:T(4,128)S(1)} %log_add_fusion.11, pred[512,2048]{0,1:T(8,128)(4,1)S(1)} %copy-done.3, bf16[2,2048,1,128]{3,1,2,0:T(8,128)(2,1)S(1)} %copy-done.15, s32[]{:T(128)S(6)} %copy.272, ...), kind=kOutput, calls=%fused_computation.16.clone.1 | convolution fusion | flops 1098907648 | bytes 27280896 | tf_op jit(solution)/shard_map/while/body/eval_jaxpr/isrd,jsd->srij/dot_general | solution.py:42
  450.1 5.0 fusion.227
  455.1 2.1 fusion.219
  457.2 3.1 copy.255
  460.4 2.3 copy.257
  462.7 3.6 copy.256
  475.3 2.1 fusion.208
  479.6 2.6 fusion.209
  487.9 2.2 exponential_reduce_fusion.9
  490.1 4.4 fusion.221
  494.5 3.9 fusion.212
  502.6 2.2 fusion.214
  504.9 2.7 exponential_reduce_fusion.10
  507.6 6.0 fusion.222
  513.6 5.7 fusion.215
  519.3 4.4 fusion.226
  523.7 2.9 fusion.216
  526.6 4.8 fusion.217
  531.4 3.8 exponential_reduce_fusion.11
  537.2 11.9 %fusion.223 = f32[1,2048,1,128]{1,3,2,0:T(8,128)} fusion(f32[2048,1,128]{0,2,1:T(8,128)} %fusion.222, f32[2048,512,4]{1,0,2:T(8,128)} %copy-done, f32[4,512]{1,0:T(4,128)S(1)} %log_add_fusion.11, pred[512,2048]{0,1:T(8,128)(4,1)S(1)} %copy-done.3, bf16[2,2048,4,128]{3,1,2,0:T(8,128)(2,1)} %get-tuple-element.461, s32[]{:T(128)S(6)} %copy.272, ...), kind=kOutput, calls=%fused_computation.58.clone.1 | convolution fusion | flops 1090781184 | bytes 20455432 | tf_op jit(solution)/shard_map/while/body/eval_jaxpr/srij,isrd->jsd/dot_general | solution.py:39
  549.1 9.0 %fusion.218 = bf16[4,512,2048]{1,2,0:T(8,128)(2,1)S(1)} fusion(f32[2048,512,4]{1,0,2:T(8,128)} %copy-done, f32[4,512]{1,0:T(4,128)S(1)} %get-tuple-element.420, f32[4,512]{1,0:T(4,128)S(1)} %log_add_fusion.11, pred[512,2048]{0,1:T(8,128)(4,1)S(1)} %copy-done.3, bf16[2,2048,1,128]{3,1,2,0:T(8,128)(2,1)S(1)} %copy-done.15, s32[]{:T(128)S(6)} %copy.272, ...), kind=kOutput, calls=%fused_computation.16.clone.1 | convolution fusion | flops 1098907648 | bytes 27280896 | tf_op jit(solution)/shard_map/while/body/eval_jaxpr/isrd,jsd->srij/dot_general | solution.py:42
  558.1 5.0 fusion.227
  563.1 2.1 fusion.219
  565.3 3.1 copy.255
  568.4 2.3 copy.257
  570.7 3.6 copy.256
  585.8 52.4 %all_to_all.129 = f32[2,2048,1,128]{3,2,0,1:T(1,128)} all-to-all(f32[2,2048,1,128]{3,2,0,1:T(1,128)} %get-tuple-element.269), channel_id=1, replica_groups=mesh['dp'=4,'seq'=8] {'seq'}, dimensions={1} | all-to-all | bytes 4194304 | tf_op jit(solution)/shard_map/all_to_all | solution.py:110
  638.2 51.2 %all_to_all.130 = f32[2,2048,1,128]{3,2,0,1:T(1,128)S(1)} all-to-all(f32[2,2048,1,128]{3,2,0,1:T(1,128)S(1)} %copy-done.14), channel_id=1, replica_groups=mesh['dp'=4,'seq'=8] {'seq'}, dimensions={1} | all-to-all | bytes 4194304 | tf_op jit(solution)/shard_map/all_to_all | solution.py:109
  689.4 4.5 all-to-all-start.5
  693.9 3.4 reduce_sum.78
  702.8 83.4 %all-to-all-done.5 = bf16[2,2048,4,128]{3,2,0,1:T(4,128)(2,1)} async-done(((bf16[2,2048,4,128]{3,2,0,1:T(4,128)(2,1)}), bf16[2,2048,4,128]{3,2,0,1:T(4,128)(2,1)}, u32[]{:S(2)}, u32[]{:S(2)}) %all-to-all-start.5) | async-done | bytes 4194336 | tf_op jit(solution)/shard_map/all_to_all | solution.py:107
  786.2 5.6 copy.203
  (134 shorter events, 57.4 us)
Async XLA Ops:
  0.6 9.7 %copy-start.16 = (bf16[2,256,4,128]{3,2,1,0:T(4,128)(2,1)S(1)}, bf16[2,256,4,128]{3,2,1,0:T(4,128)(2,1)}, u32[]{:S(2)}) copy-start(bf16[2,256,4,128]{3,2,1,0:T(4,128)(2,1)} %param.32) | copy-start | bytes 1572868
  1.8 39.0 %copy-start.17 = (s32[2]{0:T(128)S(1)}, s32[2]{0:T(128)}, u32[]{:S(2)}) copy-start(s32[2]{0:T(128)} %param.35) | copy-start | bytes 28
  1.8 46.6 %copy-start.18 = (f32[2]{0:T(128)S(1)}, f32[2]{0:T(128)}, u32[]{:S(2)}) copy-start(f32[2]{0:T(128)} %constant.334.clone) | copy-start | bytes 28
  3.0 33.0 %all-to-all-start = ((bf16[2,256,8,128]{3,1,0,2:T(8,128)(2,1)}), bf16[2,256,8,128]{3,1,0,2:T(8,128)(2,1)S(1)}, u32[]{:S(2)}, u32[]{:S(2)}) async-start(bf16[2,256,8,128]{3,1,0,2:T(8,128)(2,1)} %bitcast.103), calls=%async_computation | async-start | bytes 2097152 | tf_op jit(solution)/shard_map/all_to_all | solution.py:100
  37.2 29.5 %all-to-all-start.2 = ((bf16[2,256,8,128]{3,1,0,2:T(8,128)(2,1)}), bf16[2,256,8,128]{3,1,0,2:T(8,128)(2,1)S(1)}, u32[]{:S(2)}, u32[]{:S(2)}) async-start(bf16[2,256,8,128]{3,1,0,2:T(8,128)(2,1)} %bitcast.628), calls=%async_computation.2 | async-start | bytes 2097152 | tf_op jit(solution)/shard_map/all_to_all | solution.py:101
  66.8 10.4 %copy-start.11 = (bf16[2,256,8,128]{3,1,0,2:T(8,128)(2,1)}, bf16[2,256,8,128]{3,1,0,2:T(8,128)(2,1)S(1)}, u32[]{:S(2)}) copy-start(bf16[2,256,8,128]{3,1,0,2:T(8,128)(2,1)S(1)} %all-to-all-done.2) | copy-start | bytes 3145732
  66.8 97.1 %all-to-all-start.3 = ((bf16[2,256,32,128]{3,1,0,2:T(8,128)(2,1)}), bf16[2,256,32,128]{3,1,0,2:T(8,128)(2,1)}, u32[]{:S(2)}, u32[]{:S(2)}) async-start(bf16[2,256,32,128]{3,1,0,2:T(8,128)(2,1)} %multiply_convert_fusion), calls=%async_computation.3 | async-start | bytes 8388608 | tf_op jit(solution)/shard_map/all_to_all | solution.py:98
  163.9 97.1 %all-to-all-start.1 = ((bf16[2,256,32,128]{3,1,0,2:T(8,128)(2,1)}), bf16[2,256,32,128]{3,1,0,2:T(8,128)(2,1)}, u32[]{:S(2)}, u32[]{:S(2)}) async-start(bf16[2,256,32,128]{3,1,0,2:T(8,128)(2,1)} %copy.192), calls=%async_computation.1 | async-start | bytes 8388608 | tf_op jit(solution)/shard_map/all_to_all | solution.py:97
  261.0 97.1 %all-to-all-start.4 = ((bf16[2,256,32,128]{3,1,0,2:T(8,128)(2,1)}), bf16[2,256,32,128]{3,1,0,2:T(8,128)(2,1)}, u32[]{:S(2)}, u32[]{:S(2)}) async-start(bf16[2,256,32,128]{3,1,0,2:T(8,128)(2,1)} %copy.198), calls=%async_computation.4 | async-start | bytes 8388608 | tf_op jit(solution)/shard_map/all_to_all | solution.py:99
  364.3 30.1 %copy-start.6 = (bf16[2,2048,1,128]{3,1,2,0:T(8,128)(2,1)}, bf16[2,2048,1,128]{3,1,2,0:T(8,128)(2,1)S(1)}, u32[]{:S(2)}) copy-start(bf16[2,2048,1,128]{3,1,2,0:T(8,128)(2,1)S(1)} %get-tuple-element.458) | copy-start | bytes 3145732 | tf_op jit(solution)/shard_map/while
  365.4 34.0 %copy-start.9 = (pred[512,1536]{0,1:T(8,128)(4,1)}, pred[512,1536]{0,1:T(8,128)(4,1)S(1)}, u32[]{:S(2)}) copy-start(pred[512,1536]{0,1:T(8,128)(4,1)S(1)} %iota_compare_fusion.10) | copy-start | bytes 2359300 | tf_op jit(solution)/shard_map/while
  367.2 3.0 copy-start.10
  371.6 2.6 copy-start.5
  391.8 1.0 copy-start.1
  415.7 2.9 copy-start.3
  423.4 5.7 copy-start
  429.1 11.9 %copy-start.15 = (bf16[2,2048,1,128]{3,1,2,0:T(8,128)(2,1)S(1)}, bf16[2,2048,1,128]{3,1,2,0:T(8,128)(2,1)}, u32[]{:S(2)}) copy-start(bf16[2,2048,1,128]{3,1,2,0:T(8,128)(2,1)} %get-tuple-element.460) | copy-start | bytes 3145732 | tf_op jit(solution)/shard_map/while
  441.0 9.0 %copy-start.2 = (f32[2048,1,128]{0,2,1:T(8,128)S(1)}, f32[2048,1,128]{0,2,1:T(8,128)}, u32[]{:S(2)}) copy-start(f32[2048,1,128]{0,2,1:T(8,128)} %fusion.226) | copy-start | bytes 3145732 | tf_op jit(solution)/shard_map/while
  450.1 5.0 copy-start.7
  466.3 1.7 copy-start.4
  466.3 2.7 copy-start.12
  469.0 3.1 copy-start.8
  470.8 1.3 copy-start.13
  472.3 30.3 %copy-start.6 = (bf16[2,2048,1,128]{3,1,2,0:T(8,128)(2,1)}, bf16[2,2048,1,128]{3,1,2,0:T(8,128)(2,1)S(1)}, u32[]{:S(2)}) copy-start(bf16[2,2048,1,128]{3,1,2,0:T(8,128)(2,1)S(1)} %get-tuple-element.458) | copy-start | bytes 3145732 | tf_op jit(solution)/shard_map/while
  473.4 34.2 %copy-start.9 = (pred[512,1536]{0,1:T(8,128)(4,1)}, pred[512,1536]{0,1:T(8,128)(4,1)S(1)}, u32[]{:S(2)}) copy-start(pred[512,1536]{0,1:T(8,128)(4,1)S(1)} %iota_compare_fusion.10) | copy-start | bytes 2359300 | tf_op jit(solution)/shard_map/while
  475.3 3.0 copy-start.10
  479.6 2.6 copy-start.5
  500.0 1.0 copy-start.1
  523.7 2.9 copy-start.3
  531.4 5.7 copy-start
  537.1 11.9 %copy-start.15 = (bf16[2,2048,1,128]{3,1,2,0:T(8,128)(2,1)S(1)}, bf16[2,2048,1,128]{3,1,2,0:T(8,128)(2,1)}, u32[]{:S(2)}) copy-start(bf16[2,2048,1,128]{3,1,2,0:T(8,128)(2,1)} %get-tuple-element.460) | copy-start | bytes 3145732 | tf_op jit(solution)/shard_map/while
  549.1 9.0 %copy-start.2 = (f32[2048,1,128]{0,2,1:T(8,128)S(1)}, f32[2048,1,128]{0,2,1:T(8,128)}, u32[]{:S(2)}) copy-start(f32[2048,1,128]{0,2,1:T(8,128)} %fusion.226) | copy-start | bytes 3145732 | tf_op jit(solution)/shard_map/while
  558.1 5.0 copy-start.7
  574.3 1.7 copy-start.4
  574.3 2.7 copy-start.12
  577.0 3.1 copy-start.8
  578.8 1.3 copy-start.13
  585.8 52.4 %copy-start.14 = (f32[2,2048,1,128]{3,2,0,1:T(1,128)S(1)}, f32[2,2048,1,128]{3,2,0,1:T(1,128)}, u32[]{:S(2)}) copy-start(f32[2,2048,1,128]{3,2,0,1:T(1,128)} %get-tuple-element.268) | copy-start | bytes 6291460
  689.4 96.8 %all-to-all-start.5 = ((bf16[2,2048,4,128]{3,2,0,1:T(4,128)(2,1)}), bf16[2,2048,4,128]{3,2,0,1:T(4,128)(2,1)}, u32[]{:S(2)}, u32[]{:S(2)}) async-start(bf16[2,2048,4,128]{3,2,0,1:T(4,128)(2,1)} %get-tuple-element.267), calls=%async_computation.5 | async-start | bytes 8388608 | tf_op jit(solution)/shard_map/all_to_all | solution.py:107
where the time goes:
time: 801 us; the launch traced here: 792 us
  waiting for transfers between devices  376 us (47%)
  matrix products  149 us (19%)
  blocking collectives  109 us (14%)
  local copies, waits for them, and re-layouts  77.2 us (10%)
  other arithmetic  42.7 us (5%)
  starting transfers between devices  29.1 us (4%)
    all_to_all x1, waiting for transfers between devices, body(): lax.all_to_all(query, 'seq', split_axis=2, concat_axis=1, tiled=True)  86.7 us
    all_to_all x1, waiting for transfers between devices, body(): lax.all_to_all(scaled, 'seq', split_axis=2, concat_axis=1, tiled=True)  86.7 us
    all_to_all x1, waiting for transfers between devices, body(): lax.all_to_all(query_heads, 'seq', split_axis=1, concat_axis=2, tiled=True)  83.4 us
    all_to_all x1, waiting for transfers between devices, body(): lax.all_to_all(output, 'seq', split_axis=2, concat_axis=1, tiled=True)  80.9 us
    all_to_all x1, blocking collectives, body(): lax.all_to_all(value_heads, 'seq', split_axis=1, concat_axis=2, tiled=True)  52.4 us
    all_to_all x1, blocking collectives, body(): lax.all_to_all(key_heads, 'seq', split_axis=1, concat_axis=2, tiled=True)  51.2 us
    dot_general x8, matrix products, one_block(): jnp.einsum('srij,isrd->jsd', prob_low, g_block, preferred_element_type=jn...  47.3 us
    dot_general x8, matrix products, one_block(): jnp.einsum('isrd,jsd->srij', g_block, value_pre, preferred_element_type=j...  42.4 us
  transfers between devices with their start and end apart: 6, of which 6 were waited for; matrix products, arithmetic and copies ran while one was open for 5% of the time, Pallas kernels for 0%

commit v1 on v0

--- a/solution.py
+++ b/solution.py
@@ -1,8 +1,18 @@
+import functools
 import math
 import jax
 import jax.numpy as jnp
 from jax import lax
 from jax.sharding import PartitionSpec as P
+
+
+def _solve_keys(here_x, row_dim, array_dim):
+    found_now = jnp.stack(jnp.split(here_x, jax.lax.axis_size("seq"), axis=row_dim))
+    upper = jnp.concatenate(jax.lax.all_to_all(found_now, "seq", 0, 0), axis=array_dim)
+    return upper
+
+
+list_files = functools.partial(_solve_keys, row_dim=2, array_dim=1)
 
 
 def sequence_grads(query, scaled, keys, values, delta, length):
@@ -94,7 +104,7 @@
     key_slots = jnp.repeat(keys, copies, axis=2)
     value_slots = jnp.repeat(values, copies, axis=2)
     q_heads, g_heads, o_heads, k_heads, v_heads = (
-        lax.all_to_all(query, "seq", split_axis=2, concat_axis=1, tiled=True),
+        list_files(query),
         lax.all_to_all(scaled, "seq", split_axis=2, concat_axis=1, tiled=True),
         lax.all_to_all(output, "seq", split_axis=2, concat_axis=1, tiled=True),
         lax.all_to_all(key_slots, "seq", split_axis=2, concat_axis=1, tiled=True),

time: 801 us -> 801 us (level)
  waiting for transfers between devices: 376 us -> 362 us
  local copies, waits for them, and re-layouts: 77.2 us -> 89.8 us
    unnamed x18 -> x24, local copies, waits for them, and re-layouts: 16.4 us -> 26.2 us
  transfers between devices with their start and end apart: 6 -> 6, of which waited for: 6 -> 6; matrix products, arithmetic and copies ran while one was open for 5% -> 7% of each run, Pallas kernels for 0% -> 0%
where the time goes in v1:
time: 801 us; the launch traced here: 791 us
  waiting for transfers between devices  362 us (45%)
  matrix products  149 us (19%)
  blocking collectives  109 us (14%)
  local copies, waits for them, and re-layouts  89.8 us (11%)
  other arithmetic  42.8 us (5%)
  starting transfers between devices  29.1 us (4%)
    all_to_all x1, waiting for transfers between devices, body(): lax.all_to_all(scaled, 'seq', split_axis=2, concat_axis=1, tiled=True)  86.8 us
    all_to_all x1, waiting for transfers between devices, body(): lax.all_to_all(query_heads, 'seq', split_axis=1, concat_axis=2, tiled=True)  83.4 us
    all_to_all x1, waiting for transfers between devices, _solve_keys(): jax.lax.all_to_all(found_now, 'seq', 0, 0)  79.6 us
    all_to_all x1, waiting for transfers between devices, body(): lax.all_to_all(output, 'seq', split_axis=2, concat_axis=1, tiled=True)  74.7 us
    all_to_all x1, blocking collectives, body(): lax.all_to_all(value_heads, 'seq', split_axis=1, concat_axis=2, tiled=True)  52.4 us
    all_to_all x1, blocking collectives, body(): lax.all_to_all(key_heads, 'seq', split_axis=1, concat_axis=2, tiled=True)  51.2 us
    dot_general x8, matrix products, one_block(): jnp.einsum('srij,isrd->jsd', prob_low, g_block, preferred_element_type=jn...  47.3 us
    dot_general x8, matrix products, one_block(): jnp.einsum('isrd,jsd->srij', g_block, value_pre, preferred_element_type=j...  42.4 us
  transfers between devices with their start and end apart: 6, of which 6 were waited for; matrix products, arithmetic and copies ran while one was open for 7% of the time, Pallas kernels for 0%

profile of v1, /device:TPU:0, one launch (start us, length us, event | category | flops | bytes accessed | tf_op | source)
XLA Modules:
  0.0 791.0 jit_solution(15151187246892380342)
XLA Ops:
  3.0 7.3 all-to-all-start
  10.4 25.7 %all-to-all-done = bf16[2,256,8,128]{3,1,0,2:T(8,128)(2,1)S(1)} async-done(((bf16[2,256,8,128]{3,1,0,2:T(8,128)(2,1)}), bf16[2,256,8,128]{3,1,0,2:T(8,128)(2,1)S(1)}, u32[]{:S(2)}, u32[]{:S(2)}) %all-to-all-start) | async-done | bytes 1048608 | tf_op jit(solution)/shard_map/all_to_all | solution.py:110
  37.3 3.6 all-to-all-start.2
  41.5 5.6 psum.7
  48.5 5.9 multiply_convert_fusion
  54.5 12.3 %all-to-all-done.2 = bf16[2,256,8,128]{3,1,0,2:T(8,128)(2,1)S(1)} async-done(((bf16[2,256,8,128]{3,1,0,2:T(8,128)(2,1)}), bf16[2,256,8,128]{3,1,0,2:T(8,128)(2,1)S(1)}, u32[]{:S(2)}, u32[]{:S(2)}) %all-to-all-start.2) | async-done | bytes 1048608 | tf_op jit(solution)/shard_map/all_to_all | solution.py:111
  66.8 4.5 all-to-all-start.3
  71.3 5.8 copy.194
  77.1 86.8 %all-to-all-done.3 = bf16[2,256,32,128]{3,1,0,2:T(8,128)(2,1)} async-done(((bf16[2,256,32,128]{3,1,0,2:T(8,128)(2,1)}), bf16[2,256,32,128]{3,1,0,2:T(8,128)(2,1)}, u32[]{:S(2)}, u32[]{:S(2)}) %all-to-all-start.3) | async-done | bytes 4194336 | tf_op jit(solution)/shard_map/all_to_all | solution.py:108
  163.9 4.5 all-to-all-start.4
  168.5 2.2 bitcast_dynamic-update-slice_fusion.7
  170.6 2.3 bitcast_dynamic-update-slice_fusion.6
  175.1 2.3 bitcast_dynamic-update-slice_fusion.4
  179.6 2.3 bitcast_dynamic-update-slice_fusion.2
  184.1 2.3 bitcast_dynamic-update-slice_fusion
  186.3 74.7 %all-to-all-done.4 = bf16[2,256,32,128]{3,1,0,2:T(8,128)(2,1)} async-done(((bf16[2,256,32,128]{3,1,0,2:T(8,128)(2,1)}), bf16[2,256,32,128]{3,1,0,2:T(8,128)(2,1)}, u32[]{:S(2)}, u32[]{:S(2)}) %all-to-all-start.4) | async-done | bytes 4194336 | tf_op jit(solution)/shard_map/all_to_all | solution.py:109
  261.0 4.6 all-to-all-start.1
  265.8 2.3 copy.191
  268.1 4.6 copy.193
  272.7 5.7 fusion.155
  278.5 79.6 %all-to-all-done.1 = bf16[8,2,256,4,128]{4,3,2,1,0:T(4,128)(2,1)} async-done(((bf16[8,2,256,4,128]{4,3,2,1,0:T(4,128)(2,1)}), bf16[8,2,256,4,128]{4,3,2,1,0:T(4,128)(2,1)}, u32[]{:S(2)}, u32[]{:S(2)}) %all-to-all-start.1) | async-done | bytes 4194336 | tf_op jit(solution)/shard_map/all_to_all | solution.py:11
  358.1 5.2 copy.189
  363.3 221.5 %while.27 = (s32[]{:T(128)}, bf16[2,2048,4,128]{3,2,0,1:T(4,128)(2,1)}, f32[2,2048,1,128]{3,2,0,1:T(1,128)}, f32[2,2048,1,128]{3,2,0,1:T(1,128)}, bf16[2,2048,1,...) while((s32[]{:T(128)}, ...), condition=%wide.region_12.13_spmd, body=%wide.region_3.12_spmd.sunk | while | flops 13606184960 | bytes 444718720 | solution.py:114
  370.6 2.6 fusion.209
  380.9 4.4 fusion.221
  385.3 3.9 fusion.212
  393.4 2.2 fusion.214
  395.7 2.7 exponential_reduce_fusion.10
  398.4 6.2 fusion.222
  404.7 5.7 fusion.215
  410.3 4.4 fusion.226
  414.7 2.9 fusion.216
  417.7 4.8 fusion.217
  422.5 3.8 exponential_reduce_fusion.11
  428.2 11.9 %fusion.223 = f32[1,2048,1,128]{1,3,2,0:T(8,128)} fusion(f32[2048,1,128]{0,2,1:T(8,128)} %fusion.222, f32[2048,512,4]{1,0,2:T(8,128)} %copy-done, f32[4,512]{1,0:T(4,128)S(1)} %log_add_fusion.11, pred[512,2048]{0,1:T(8,128)(4,1)S(1)} %copy-done.3, bf16[2,2048,4,128]{3,1,2,0:T(8,128)(2,1)} %get-tuple-element.461, s32[]{:T(128)S(6)} %copy.275, ...), kind=kOutput, calls=%fused_computation.58.clone.1 | convolution fusion | flops 1090781184 | bytes 20455432 | tf_op jit(solution)/shard_map/while/body/eval_jaxpr/srij,isrd->jsd/dot_general | solution.py:49
  440.1 9.0 %fusion.218 = bf16[4,512,2048]{1,2,0:T(8,128)(2,1)S(1)} fusion(f32[2048,512,4]{1,0,2:T(8,128)} %copy-done, f32[4,512]{1,0:T(4,128)S(1)} %get-tuple-element.420, f32[4,512]{1,0:T(4,128)S(1)} %log_add_fusion.11, pred[512,2048]{0,1:T(8,128)(4,1)S(1)} %copy-done.3, bf16[2,2048,1,128]{3,1,2,0:T(8,128)(2,1)S(1)} %copy-done.15, s32[]{:T(128)S(6)} %copy.275, ...), kind=kOutput, calls=%fused_computation.16.clone.1 | convolution fusion | flops 1098907648 | bytes 27280896 | tf_op jit(solution)/shard_map/while/body/eval_jaxpr/isrd,jsd->srij/dot_general | solution.py:52
  449.1 5.0 fusion.227
  456.3 3.1 copy.251
  459.4 2.3 copy.253
  461.7 3.6 copy.252
  478.6 2.6 fusion.209
  486.9 2.2 exponential_reduce_fusion.9
  489.2 4.4 fusion.221
  493.5 3.9 fusion.212
  501.7 2.2 fusion.214
  503.9 2.7 exponential_reduce_fusion.10
  506.7 6.0 fusion.222
  512.6 5.7 fusion.215
  518.3 4.4 fusion.226
  522.7 2.9 fusion.216
  525.7 4.8 fusion.217
  530.5 3.8 exponential_reduce_fusion.11
  536.2 11.9 %fusion.223 = f32[1,2048,1,128]{1,3,2,0:T(8,128)} fusion(f32[2048,1,128]{0,2,1:T(8,128)} %fusion.222, f32[2048,512,4]{1,0,2:T(8,128)} %copy-done, f32[4,512]{1,0:T(4,128)S(1)} %log_add_fusion.11, pred[512,2048]{0,1:T(8,128)(4,1)S(1)} %copy-done.3, bf16[2,2048,4,128]{3,1,2,0:T(8,128)(2,1)} %get-tuple-element.461, s32[]{:T(128)S(6)} %copy.275, ...), kind=kOutput, calls=%fused_computation.58.clone.1 | convolution fusion | flops 1090781184 | bytes 20455432 | tf_op jit(solution)/shard_map/while/body/eval_jaxpr/srij,isrd->jsd/dot_general | solution.py:49
  548.1 9.0 %fusion.218 = bf16[4,512,2048]{1,2,0:T(8,128)(2,1)S(1)} fusion(f32[2048,512,4]{1,0,2:T(8,128)} %copy-done, f32[4,512]{1,0:T(4,128)S(1)} %get-tuple-element.420, f32[4,512]{1,0:T(4,128)S(1)} %log_add_fusion.11, pred[512,2048]{0,1:T(8,128)(4,1)S(1)} %copy-done.3, bf16[2,2048,1,128]{3,1,2,0:T(8,128)(2,1)S(1)} %copy-done.15, s32[]{:T(128)S(6)} %copy.275, ...), kind=kOutput, calls=%fused_computation.16.clone.1 | convolution fusion | flops 1098907648 | bytes 27280896 | tf_op jit(solution)/shard_map/while/body/eval_jaxpr/isrd,jsd->srij/dot_general | solution.py:52
  557.2 5.0 fusion.227
  564.3 3.1 copy.251
  567.4 2.3 copy.253
  569.8 3.6 copy.252
  584.8 52.4 %all_to_all.116 = f32[2,2048,1,128]{3,2,0,1:T(1,128)} all-to-all(f32[2,2048,1,128]{3,2,0,1:T(1,128)} %get-tuple-element.269), channel_id=1, replica_groups=mesh['dp'=4,'seq'=8] {'seq'}, dimensions={1} | all-to-all | bytes 4194304 | tf_op jit(solution)/shard_map/all_to_all | solution.py:120
  637.2 51.2 %all_to_all.117 = f32[2,2048,1,128]{3,2,0,1:T(1,128)S(1)} all-to-all(f32[2,2048,1,128]{3,2,0,1:T(1,128)S(1)} %copy-done.14), channel_id=1, replica_groups=mesh['dp'=4,'seq'=8] {'seq'}, dimensions={1} | all-to-all | bytes 4194304 | tf_op jit(solution)/shard_map/all_to_all | solution.py:119
  688.4 4.5 all-to-all-start.5
  693.0 3.4 reduce_sum.78
  701.8 83.4 %all-to-all-done.5 = bf16[2,2048,4,128]{3,2,0,1:T(4,128)(2,1)} async-done(((bf16[2,2048,4,128]{3,2,0,1:T(4,128)(2,1)}), bf16[2,2048,4,128]{3,2,0,1:T(4,128)(2,1)}, u32[]{:S(2)}, u32[]{:S(2)}) %all-to-all-start.5) | async-done | bytes 4194336 | tf_op jit(solution)/shard_map/all_to_all | solution.py:117
  785.3 5.6 copy.199
  (141 shorter events, 72.3 us)
Async XLA Ops:
  0.6 9.7 %copy-start.16 = (bf16[2,256,4,128]{3,2,1,0:T(4,128)(2,1)S(1)}, bf16[2,256,4,128]{3,2,1,0:T(4,128)(2,1)}, u32[]{:S(2)}) copy-start(bf16[2,256,4,128]{3,2,1,0:T(4,128)(2,1)} %param.32) | copy-start | bytes 1572868
  1.8 39.0 %copy-start.17 = (s32[2]{0:T(128)S(1)}, s32[2]{0:T(128)}, u32[]{:S(2)}) copy-start(s32[2]{0:T(128)} %param.35) | copy-start | bytes 28
  1.8 46.6 %copy-start.18 = (f32[2]{0:T(128)S(1)}, f32[2]{0:T(128)}, u32[]{:S(2)}) copy-start(f32[2]{0:T(128)} %constant.334.clone) | copy-start | bytes 28
  3.0 33.0 %all-to-all-start = ((bf16[2,256,8,128]{3,1,0,2:T(8,128)(2,1)}), bf16[2,256,8,128]{3,1,0,2:T(8,128)(2,1)S(1)}, u32[]{:S(2)}, u32[]{:S(2)}) async-start(bf16[2,256,8,128]{3,1,0,2:T(8,128)(2,1)} %bitcast.103), calls=%async_computation | async-start | bytes 2097152 | tf_op jit(solution)/shard_map/all_to_all | solution.py:110
  37.3 29.5 %all-to-all-start.2 = ((bf16[2,256,8,128]{3,1,0,2:T(8,128)(2,1)}), bf16[2,256,8,128]{3,1,0,2:T(8,128)(2,1)S(1)}, u32[]{:S(2)}, u32[]{:S(2)}) async-start(bf16[2,256,8,128]{3,1,0,2:T(8,128)(2,1)} %bitcast.642), calls=%async_computation.2 | async-start | bytes 2097152 | tf_op jit(solution)/shard_map/all_to_all | solution.py:111
  66.8 10.3 %copy-start.11 = (bf16[2,256,8,128]{3,1,0,2:T(8,128)(2,1)}, bf16[2,256,8,128]{3,1,0,2:T(8,128)(2,1)S(1)}, u32[]{:S(2)}) copy-start(bf16[2,256,8,128]{3,1,0,2:T(8,128)(2,1)S(1)} %all-to-all-done.2) | copy-start | bytes 3145732
  66.8 97.1 %all-to-all-start.3 = ((bf16[2,256,32,128]{3,1,0,2:T(8,128)(2,1)}), bf16[2,256,32,128]{3,1,0,2:T(8,128)(2,1)}, u32[]{:S(2)}, u32[]{:S(2)}) async-start(bf16[2,256,32,128]{3,1,0,2:T(8,128)(2,1)} %multiply_convert_fusion), calls=%async_computation.3 | async-start | bytes 8388608 | tf_op jit(solution)/shard_map/all_to_all | solution.py:108
  163.9 97.1 %all-to-all-start.4 = ((bf16[2,256,32,128]{3,1,0,2:T(8,128)(2,1)}), bf16[2,256,32,128]{3,1,0,2:T(8,128)(2,1)}, u32[]{:S(2)}, u32[]{:S(2)}) async-start(bf16[2,256,32,128]{3,1,0,2:T(8,128)(2,1)} %copy.194), calls=%async_computation.4 | async-start | bytes 8388608 | tf_op jit(solution)/shard_map/all_to_all | solution.py:109
  261.0 97.1 %all-to-all-start.1 = ((bf16[8,2,256,4,128]{4,3,2,1,0:T(4,128)(2,1)}), bf16[8,2,256,4,128]{4,3,2,1,0:T(4,128)(2,1)}, u32[]{:S(2)}, u32[]{:S(2)}) async-start(bf16[8,2,256,4,128]{4,3,2,1,0:T(4,128)(2,1)} %bitcast_dynamic-update-slice_fusion), calls=%async_computation.1 | async-start | bytes 8388608 | tf_op jit(solution)/shard_map/all_to_all | solution.py:11
  363.3 30.1 %copy-start.6 = (bf16[2,2048,1,128]{3,1,2,0:T(8,128)(2,1)}, bf16[2,2048,1,128]{3,1,2,0:T(8,128)(2,1)S(1)}, u32[]{:S(2)}) copy-start(bf16[2,2048,1,128]{3,1,2,0:T(8,128)(2,1)S(1)} %get-tuple-element.458) | copy-start | bytes 3145732 | tf_op jit(solution)/shard_map/while
  364.5 34.0 %copy-start.9 = (pred[512,1536]{0,1:T(8,128)(4,1)}, pred[512,1536]{0,1:T(8,128)(4,1)S(1)}, u32[]{:S(2)}) copy-start(pred[512,1536]{0,1:T(8,128)(4,1)S(1)} %iota_compare_fusion.10) | copy-start | bytes 2359300 | tf_op jit(solution)/shard_map/while
  366.3 3.0 copy-start.10
  370.6 2.6 copy-start.5
  390.8 1.0 copy-start.1
  414.7 2.9 copy-start.3
  422.5 5.7 copy-start
  428.2 11.9 %copy-start.15 = (bf16[2,2048,1,128]{3,1,2,0:T(8,128)(2,1)S(1)}, bf16[2,2048,1,128]{3,1,2,0:T(8,128)(2,1)}, u32[]{:S(2)}) copy-start(bf16[2,2048,1,128]{3,1,2,0:T(8,128)(2,1)} %get-tuple-element.460) | copy-start | bytes 3145732 | tf_op jit(solution)/shard_map/while
  440.1 9.0 %copy-start.2 = (f32[2048,1,128]{0,2,1:T(8,128)S(1)}, f32[2048,1,128]{0,2,1:T(8,128)}, u32[]{:S(2)}) copy-start(f32[2048,1,128]{0,2,1:T(8,128)} %fusion.226) | copy-start | bytes 3145732 | tf_op jit(solution)/shard_map/while
  449.1 5.0 copy-start.7
  465.3 1.7 copy-start.4
  465.3 2.7 copy-start.12
  468.0 3.1 copy-start.8
  469.8 1.3 copy-start.13
  471.3 30.3 %copy-start.6 = (bf16[2,2048,1,128]{3,1,2,0:T(8,128)(2,1)}, bf16[2,2048,1,128]{3,1,2,0:T(8,128)(2,1)S(1)}, u32[]{:S(2)}) copy-start(bf16[2,2048,1,128]{3,1,2,0:T(8,128)(2,1)S(1)} %get-tuple-element.458) | copy-start | bytes 3145732 | tf_op jit(solution)/shard_map/while
  472.5 34.2 %copy-start.9 = (pred[512,1536]{0,1:T(8,128)(4,1)}, pred[512,1536]{0,1:T(8,128)(4,1)S(1)}, u32[]{:S(2)}) copy-start(pred[512,1536]{0,1:T(8,128)(4,1)S(1)} %iota_compare_fusion.10) | copy-start | bytes 2359300 | tf_op jit(solution)/shard_map/while
  474.3 3.0 copy-start.10
  478.6 2.6 copy-start.5
  499.1 1.0 copy-start.1
  522.7 2.9 copy-start.3
  530.5 5.7 copy-start
  536.2 11.9 %copy-start.15 = (bf16[2,2048,1,128]{3,1,2,0:T(8,128)(2,1)S(1)}, bf16[2,2048,1,128]{3,1,2,0:T(8,128)(2,1)}, u32[]{:S(2)}) copy-start(bf16[2,2048,1,128]{3,1,2,0:T(8,128)(2,1)} %get-tuple-element.460) | copy-start | bytes 3145732 | tf_op jit(solution)/shard_map/while
  548.1 9.0 %copy-start.2 = (f32[2048,1,128]{0,2,1:T(8,128)S(1)}, f32[2048,1,128]{0,2,1:T(8,128)}, u32[]{:S(2)}) copy-start(f32[2048,1,128]{0,2,1:T(8,128)} %fusion.226) | copy-start | bytes 3145732 | tf_op jit(solution)/shard_map/while
  557.1 5.0 copy-start.7
  573.4 1.7 copy-start.4
  573.4 2.7 copy-start.12
  576.0 3.1 copy-start.8
  577.9 1.3 copy-start.13
  584.8 52.4 %copy-start.14 = (f32[2,2048,1,128]{3,2,0,1:T(1,128)S(1)}, f32[2,2048,1,128]{3,2,0,1:T(1,128)}, u32[]{:S(2)}) copy-start(f32[2,2048,1,128]{3,2,0,1:T(1,128)} %get-tuple-element.268) | copy-start | bytes 6291460
  688.4 96.8 %all-to-all-start.5 = ((bf16[2,2048,4,128]{3,2,0,1:T(4,128)(2,1)}), bf16[2,2048,4,128]{3,2,0,1:T(4,128)(2,1)}, u32[]{:S(2)}, u32[]{:S(2)}) async-start(bf16[2,2048,4,128]{3,2,0,1:T(4,128)(2,1)} %get-tuple-element.267), calls=%async_computation.5 | async-start | bytes 8388608 | tf_op jit(solution)/shard_map/all_to_all | solution.py:117
